TPU v7x, 512 devices: a whole 4x8x8 slice. The times are simulated.
512 devices in a mesh: row: 32 (over x_lo, y, core), col: 16 (over z, x_hi).
Axes of the slice: x: 4 (x_hi: 2, x_lo: 2; x = x_hi * 2 + x_lo), y: 8, z: 8, core: 2. Of those that a mesh axis runs over, the one named last changes fastest.
Arguments:
- support: bfloat16 [131072, 4096], P(('row', 'col')), may hold values from -6 to 6
- targets: bfloat16 [1024, 4096], P('col'), may hold values from -6 to 6
- panels: float32 [2, 128, 131072], P(None, None, ('row', 'col')), may hold values from -0.21875 to 0.21875
- diag_inverses: float32 [2, 128, 128], replicated, may hold values from -1 to 1.5, as said below
Outputs:
- solved: float32 [1024, 131072], P('col', 'row')
Inputs may be any that keep to these rules, and one draw needn't show every extreme that they name: Each diag_inverses[k] is lower triangular.
All inputs are finite; a program needn't handle non-finite values.
Results may differ from a plain program's by a relative error of at most 0.0003.
Values may be sent and summed in bfloat16 or wider, within the bound.
A program may use at most 64 MiB of HBM per device.

v0:
```python
import math
import jax
import jax.numpy as jnp
from jax import lax
from jax.sharding import PartitionSpec as P


def spread(value, axis, root):
    mine = lax.axis_index(axis) == root
    return lax.psum(jnp.where(mine, value, jnp.zeros_like(value)), axis)


def solve_head(pivot_cols, inverse):
    return jnp.dot(
        pivot_cols, inverse.T, precision=lax.Precision.HIGHEST, preferred_element_type=jnp.float32
    )


def apply_panel(current, solved_head, panel_cols):
    return current - jnp.dot(
        solved_head, panel_cols, precision=lax.Precision.HIGHEST, preferred_element_type=jnp.float32
    )


def shards(support, targets, panels, diag_inverses):
    feature_width = support.shape[1]
    kernel_scale = 0.5 / math.sqrt(feature_width)
    pivot_width = diag_inverses.shape[1]
    row_pos = lax.axis_index("row")
    products = jnp.einsum(
        "tf,sf->ts",
        lax.all_gather(targets, "col", axis=0, tiled=True),
        support,
        preferred_element_type=jnp.float32,
    )
    strip_tile = jnp.exp(kernel_scale * products)
    grid_tile = lax.all_to_all(strip_tile, "col", split_axis=0, concat_axis=1, tiled=True)
    panel_grid = lax.all_gather(panels, "col", axis=2, tiled=True)
    for panel_num in range(2):
        pivot_cols = grid_tile[:, :pivot_width]
        solved_head = spread(solve_head(pivot_cols, diag_inverses[panel_num]), "row", panel_num)
        updated = apply_panel(grid_tile, solved_head, panel_grid[panel_num])
        new_head = jnp.where(
            row_pos == panel_num,
            solved_head,
            jnp.where(row_pos < panel_num, pivot_cols, updated[:, :pivot_width]),
        )
        grid_tile = updated.at[:, :pivot_width].set(new_head)
    return grid_tile


def solution(mesh):
    in_specs = (P(("row", "col"), None), P("col", None), P(None, None, ("row", "col")), P())
    out_specs = P("col", "row")
    return jax.shard_map(shards, mesh=mesh, in_specs=in_specs, out_specs=out_specs, check_vma=False)
```

profile of v0, /device:TPU:2, one launch (start us, length us, event | category | flops | bytes accessed | tf_op | source)
XLA Modules:
  0.0 432.9 jit_solution(4030041354875455081)
XLA Ops:
  6.5 0.0 copy-start
  6.5 0.0 all-gather.3.cloned.1.call-start
  6.5 0.7 all-gather.3.cloned.1.call-update
  7.3 0.0 all-gather.5.cloned.1.call-start
  7.3 0.7 all-gather.5.cloned.1.call-update
  8.0 148.2 %all-gather.3.cloned.1.call-done = bf16[1024,4096]{1,0:T(8,128)(2,1)} async-done(((bf16[64,4096]{1,0:T(8,128)(2,1)}), bf16[1024,4096]{1,0:T(8,128)(2,1)}) %all-gather.3.cloned.1.call-update) | async-done | bytes 8388624 | tf_op jit(solution)/shard_map/all_gather | solution.py:32
  156.2 0.0 copy-done
  156.2 6.7 %fusion = f32[1024,256]{1,0:T(8,128)} fusion(bf16[1024,4096]{1,0:T(8,128)(2,1)} %all-gather.3.cloned.1.call-done, bf16[256,4096]{1,0:T(8,128)(2,1)S(1)} %copy-done), kind=kOutput, calls=%fused_computation.5 | convolution fusion | flops 2147745792 | bytes 11534336 | tf_op jit(solution)/shard_map/tf,sf->ts/dot_general | solution.py:30
  162.9 0.0 copy-start.3
  162.9 5.3 %all-to-all-start = ((f32[16,64,256]{2,1,0:T(8,128)}), f32[16,64,256]{2,1,0:T(8,128)S(1)}, u32[]{:S(2)}, u32[]{:S(2)}) async-start(f32[16,64,256]{2,1,0:T(8,128)} %bitcast.25), calls=%async_computation | async-start | bytes 2097152 | tf_op jit(solution)/shard_map/all_to_all | solution.py:37
  168.2 0.6 compare_reduce_fusion
  168.8 33.1 %all-to-all-done = f32[16,64,256]{2,1,0:T(8,128)S(1)} async-done(((f32[16,64,256]{2,1,0:T(8,128)}), f32[16,64,256]{2,1,0:T(8,128)S(1)}, u32[]{:S(2)}, u32[]{:S(2)}) %all-to-all-start) | async-done | bytes 1048608 | tf_op jit(solution)/shard_map/all_to_all | solution.py:37
  201.9 0.0 copy-start.2
  201.9 1.0 copy-done.2
  202.9 1.3 copy.6
  204.2 0.0 copy-done.3
  204.2 0.2 convolution_select_fusion.1
  204.5 106.4 %psum.14 = f32[64,128]{1,0:T(8,128)S(1)} all-reduce(f32[64,128]{1,0:T(8,128)S(1)} %convolution_select_fusion.1), channel_id=1, replica_groups=mesh['row'=32,'col'=16] {'row'}, use_global_device_ids=true, to_apply=%region_0.1 | all-reduce | flops 8192 | bytes 65536 | tf_op jit(solution)/shard_map/psum | solution.py:10
  310.9 0.0 all-gather.5.cloned.1.call-done
  310.9 2.8 convolution_subtract_fusion.1
  313.7 0.6 constant_dynamic-update-slice_fusion
  314.4 0.0 copy-start.1
  314.4 1.0 copy-done.1
  315.3 0.2 convolution_select_fusion
  315.6 104.4 %psum.15 = f32[64,128]{1,0:T(8,128)S(1)} all-reduce(f32[64,128]{1,0:T(8,128)S(1)} %convolution_select_fusion), channel_id=1, replica_groups=mesh['row'=32,'col'=16] {'row'}, use_global_device_ids=true, to_apply=%region_2.3 | all-reduce | flops 8192 | bytes 65536 | tf_op jit(solution)/shard_map/psum | solution.py:10
  420.0 4.0 convolution_subtract_fusion
  424.1 2.0 select_dynamic-update-slice_fusion
Async XLA Ops:
  6.5 149.6 %copy-start = (bf16[256,4096]{1,0:T(8,128)(2,1)S(1)}, bf16[256,4096]{1,0:T(8,128)(2,1)}, u32[]{:S(2)}) copy-start(bf16[256,4096]{1,0:T(8,128)(2,1)} %param.8) | copy-start | bytes 6291460
  6.5 149.6 %all-gather.3.cloned.1.call-start = ((), (), s32[]{:S(2)}) async-start(), calls=%async_computation.1 | async-start | bytes 8912896 | tf_op jit(solution)/shard_map/all_gather | solution.py:32
  7.3 303.6 %all-gather.5.cloned.1.call-start = ((), (), s32[]{:S(2)}) async-start(), calls=%async_computation.2 | async-start | bytes 4456448 | tf_op jit(solution)/shard_map/all_gather | solution.py:38
  162.9 41.3 %copy-start.3 = (f32[2,128,128]{2,1,0:T(8,128)S(1)}, f32[2,128,128]{2,1,0:T(8,128)}, u32[]{:S(2)}) copy-start(f32[2,128,128]{2,1,0:T(8,128)} %param.11) | copy-start | bytes 393220
  162.9 39.0 %all-to-all-start = ((f32[16,64,256]{2,1,0:T(8,128)}), f32[16,64,256]{2,1,0:T(8,128)S(1)}, u32[]{:S(2)}, u32[]{:S(2)}) async-start(f32[16,64,256]{2,1,0:T(8,128)} %bitcast.25), calls=%async_computation | async-start | bytes 2097152 | tf_op jit(solution)/shard_map/all_to_all | solution.py:37
  201.9 1.0 copy-start.2
  314.4 1.0 copy-start.1
Sparse Core Ops, SparseCore 0:
  10.5 145.5 all-gather.2
  159.2 117.2 all-gather.4
where the time goes:
time: 433 us
  blocking collectives  211 us (49%)
  waiting for transfers between devices  183 us (42%)
  matrix products  14.1 us (3%)
  between operations  13.5 us (3%)
  starting transfers between devices  5.33 us (1%)
    psum x2, blocking collectives, spread(): return lax.psum(jnp.where(mine, value, jnp.zeros_like(value)), axis)  211 us
    all_gather x1, waiting for transfers between devices, shards(): lax.all_gather(targets, 'col', axis=0, tiled=True)  148 us
    all_to_all x1, waiting for transfers between devices, shards(): lax.all_to_all(strip_tile, 'col', split_axis=0, concat_axis=1, tiled=True)  33.1 us
  transfers between devices with their start and end apart: 3, of which 2 were waited for; matrix products, arithmetic and copies ran while one was open for 2% of the time, Pallas kernels for 0%

commit v1 on v0

--- a/solution.py
+++ b/solution.py
@@ -3,11 +3,12 @@
 import jax.numpy as jnp
 from jax import lax
 from jax.sharding import PartitionSpec as P
+from jax.lax import all_gather
 
 
 def spread(value, axis, root):
     mine = lax.axis_index(axis) == root
-    return lax.psum(jnp.where(mine, value, jnp.zeros_like(value)), axis)
+    return jnp.sum(all_gather(jnp.where(mine, value, jnp.zeros_like(value)), axis), 0)
 
 
 def solve_head(pivot_cols, inverse):

time: 433 us -> 461 us (1.065)
  the two profiles are of different devices: /device:TPU:2 before, /device:TPU:1 now
where the time goes in v1:
time: 461 us; the launch traced here: 460 us
  waiting for transfers between devices  418 us (91%)
  matrix products  15.3 us (3%)
  between operations  13.2 us (3%)
  other arithmetic  5.91 us (1%)
    all_gather x1, waiting for transfers between devices, shards(): lax.all_gather(targets, 'col', axis=0, tiled=True)  150 us
    all_gather x2, waiting for transfers between devices, spread(): all_gather(jnp.where(mine, value, jnp.zeros_like(value)), axis)  131 us
    all_gather x1, waiting for transfers between devices, shards(): panel_grid = lax.all_gather(panels, 'col', axis=2, tiled=True)  110 us
    all_to_all x1, waiting for transfers between devices, shards(): lax.all_to_all(strip_tile, 'col', split_axis=0, concat_axis=1, tiled=True)  26.2 us
  transfers between devices with their start and end apart: 5, of which 5 were waited for; matrix products, arithmetic and copies ran while one was open for 0% of the time, Pallas kernels for 0%

profile of v1, /device:TPU:1, one launch (start us, length us, event | category | flops | bytes accessed | tf_op | source)
XLA Modules:
  0.0 460.3 jit_solution(15037276233325081900)
XLA Ops:
  6.5 0.0 copy-start
  6.5 0.0 all-gather.7.cloned.1.call-start
  6.5 0.7 all-gather.7.cloned.1.call-update
  7.3 150.2 %all-gather.7.cloned.1.call-done = bf16[1024,4096]{1,0:T(8,128)(2,1)} async-done(((bf16[64,4096]{1,0:T(8,128)(2,1)}), bf16[1024,4096]{1,0:T(8,128)(2,1)}) %all-gather.7.cloned.1.call-update) | async-done | bytes 8388624 | tf_op jit(solution)/shard_map/all_gather | solution.py:33
  157.5 0.0 copy-done
  157.5 6.7 %fusion = f32[1024,256]{1,0:T(8,128)} fusion(bf16[1024,4096]{1,0:T(8,128)(2,1)} %all-gather.7.cloned.1.call-done, bf16[256,4096]{1,0:T(8,128)(2,1)S(1)} %copy-done), kind=kOutput, calls=%fused_computation.5 | convolution fusion | flops 2147745792 | bytes 11534336 | tf_op jit(solution)/shard_map/tf,sf->ts/dot_general | solution.py:31
  164.2 0.0 copy-start.3
  164.2 4.1 all-to-all-start
  168.4 0.0 all-gather.11.cloned.1.call-start
  168.4 26.2 %all-to-all-done = f32[16,64,256]{2,1,0:T(8,128)S(1)} async-done(((f32[16,64,256]{2,1,0:T(8,128)}), f32[16,64,256]{2,1,0:T(8,128)S(1)}, u32[]{:S(2)}, u32[]{:S(2)}) %all-to-all-start) | async-done | bytes 1048608 | tf_op jit(solution)/shard_map/all_to_all | solution.py:38
  194.6 0.0 copy-start.2
  194.6 1.0 copy-done.2
  195.6 1.3 copy.6
  196.9 0.0 copy-done.3
  196.9 0.9 convolution_select_fusion.1
  197.8 0.0 all-gather.11.cloned.1.call-update
  197.8 0.0 all-gather.9.cloned.1.call-start
  197.9 0.7 all-gather.9.cloned.1.call-update
  198.6 0.0 all-gather.13.cloned.1.call-start
  198.6 0.7 compare_reduce_fusion
  199.3 64.6 %all-gather.11.cloned.1.call-done = f32[2048,128]{1,0:T(8,128)} async-done(((f32[64,128]{1,0:T(8,128)}), f32[2048,128]{1,0:T(8,128)}) %all-gather.11.cloned.1.call-update) | async-done | bytes 1048592 | tf_op jit(solution)/shard_map/all_gather | solution.py:11
  263.8 1.3 reduce_sum.18
  265.1 109.6 %all-gather.9.cloned.1.call-done = f32[2,128,4096]{2,1,0:T(8,128)} async-done(((f32[2,128,256]{2,1,0:T(8,128)}), f32[2,128,4096]{2,1,0:T(8,128)}) %all-gather.9.cloned.1.call-update) | async-done | bytes 4194320 | tf_op jit(solution)/shard_map/all_gather | solution.py:39
  374.7 2.8 convolution_subtract_fusion.1
  377.5 0.6 constant_dynamic-update-slice_fusion
  378.2 0.0 copy-start.1
  378.2 1.0 copy-done.1
  379.2 0.9 convolution_select_fusion
  380.0 0.0 all-gather.13.cloned.1.call-update
  380.1 66.3 %all-gather.13.cloned.1.call-done = f32[2048,128]{1,0:T(8,128)} async-done(((f32[64,128]{1,0:T(8,128)}), f32[2048,128]{1,0:T(8,128)}) %all-gather.13.cloned.1.call-update) | async-done | bytes 1048592 | tf_op jit(solution)/shard_map/all_gather | solution.py:11
  446.4 1.3 reduce_sum.19
  447.7 4.0 convolution_subtract_fusion
  451.7 2.0 select_dynamic-update-slice_fusion
Async XLA Ops:
  6.5 151.0 %copy-start = (bf16[256,4096]{1,0:T(8,128)(2,1)S(1)}, bf16[256,4096]{1,0:T(8,128)(2,1)}, u32[]{:S(2)}) copy-start(bf16[256,4096]{1,0:T(8,128)(2,1)} %param.8) | copy-start | bytes 6291460
  6.5 151.0 %all-gather.7.cloned.1.call-start = ((), (), s32[]{:S(2)}) async-start(), calls=%async_computation.1 | async-start | bytes 8912896 | tf_op jit(solution)/shard_map/all_gather | solution.py:33
  164.2 32.7 %copy-start.3 = (f32[2,128,128]{2,1,0:T(8,128)S(1)}, f32[2,128,128]{2,1,0:T(8,128)}, u32[]{:S(2)}) copy-start(f32[2,128,128]{2,1,0:T(8,128)} %param.11) | copy-start | bytes 393220
  164.2 30.4 %all-to-all-start = ((f32[16,64,256]{2,1,0:T(8,128)}), f32[16,64,256]{2,1,0:T(8,128)S(1)}, u32[]{:S(2)}, u32[]{:S(2)}) async-start(f32[16,64,256]{2,1,0:T(8,128)} %bitcast.28), calls=%async_computation | async-start | bytes 2097152 | tf_op jit(solution)/shard_map/all_to_all | solution.py:38
  168.4 95.5 %all-gather.11.cloned.1.call-start = ((), (), s32[]{:S(2)}) async-start(), calls=%async_computation.3 | async-start | bytes 1081344 | tf_op jit(solution)/shard_map/all_gather | solution.py:11
  194.6 1.0 copy-start.2
  197.8 176.9 %all-gather.9.cloned.1.call-start = ((), (), s32[]{:S(2)}) async-start(), calls=%async_computation.2 | async-start | bytes 4456448 | tf_op jit(solution)/shard_map/all_gather | solution.py:39
  198.6 247.8 %all-gather.13.cloned.1.call-start = ((), (), s32[]{:S(2)}) async-start(), calls=%async_computation.4 | async-start | bytes 1081344 | tf_op jit(solution)/shard_map/all_gather | solution.py:11
  378.2 1.0 copy-start.1
Sparse Core Ops, SparseCore 0:
  10.5 146.9 all-gather.6
  197.9 65.8 all-gather.10
  266.9 107.7 all-gather.8
  380.2 66.1 all-gather.12
